TPU v7x, 32 devices: a whole 2x2x4 slice. The times are simulated.
32 devices in a mesh: lat: 4 (over y, x), kpt: 8 (over z, core).
Axes of the slice: x: 2, y: 2, z: 4, core: 2. Of those that a mesh axis runs over, the one named last changes fastest.
Arguments:
- coarse: bfloat16 [2, 4, 32, 12288], P(None, 'lat', 'kpt'), may hold values from -1 to 1
- rp_vectors: int32 [4, 3], P('lat'), may hold values from -4 to 4
- rp_weights: int32 [4], P('lat'), may hold values from 1 to 3
- re_vectors: int32 [32, 3], replicated, may hold values from -4 to 4
- re_weights: int32 [32], replicated, may hold values from 1 to 3
- q_points: float32 [2, 3], replicated, may hold values from 0 to 1
- k_points: float32 [512, 3], P('kpt'), may hold values from 0 to 1
- modes_rot: bfloat16 [2, 2, 48, 48], replicated, may hold values from -0.625 to 0.625
- u_k: bfloat16 [2, 512, 16, 16], P(None, 'kpt'), may hold values from -1 to 1
- u_kq: bfloat16 [2, 2, 512, 16, 16], P(None, None, 'kpt'), may hold values from -1 to 1
- mask_k: int32 [512, 16], P('kpt'), may hold values 0 or 1
- mask_kq: int32 [2, 512, 16], P(None, 'kpt'), may hold values 0 or 1
Outputs:
- coupling: bfloat16 [2, 512, 2, 12288], P(None, 'kpt', None, 'lat')
All inputs are finite; a program needn't handle non-finite values. No bound on the sum of `mask_k` or of `mask_kq` on one device may be relied on, other than what follows from the above.
Results may differ from a plain program's by a relative error of at most 0.017.
Values may be sent and summed in bfloat16 or wider, within the bound.
A program may use at most 128 MiB of HBM per device.

v0:
```python
import jax
import jax.numpy as jnp
from jax import lax
from jax.sharding import PartitionSpec as P

two_pi = 6.283185307179586


def phases(points, vectors, weights):
    cells = vectors.astype(jnp.float32)
    argument = two_pi * (
        points[:, 0:1] * cells[None, :, 0]
        + points[:, 1:2] * cells[None, :, 1]
        + points[:, 2:3] * cells[None, :, 2]
    )
    inverse = 1.0 / weights.astype(jnp.float32)
    return (
        (jnp.cos(argument) * inverse).astype(jnp.bfloat16),
        (jnp.sin(argument) * inverse).astype(jnp.bfloat16),
    )


def rotate_modes(values, modes_rot):
    shape = values.shape
    mode_count = modes_rot.shape[2]
    split = values.reshape(shape[0], shape[1], shape[2], mode_count, shape[3] // mode_count)
    br = jnp.einsum(
        "qmn,qrmx->qrnx", modes_rot[0], split[0], preferred_element_type=jnp.float32
    ) - jnp.einsum("qmn,qrmx->qrnx", modes_rot[1], split[1], preferred_element_type=jnp.float32)
    bi = jnp.einsum(
        "qmn,qrmx->qrnx", modes_rot[0], split[1], preferred_element_type=jnp.float32
    ) + jnp.einsum("qmn,qrmx->qrnx", modes_rot[1], split[0], preferred_element_type=jnp.float32)
    return jnp.stack([br, bi]).reshape(shape).astype(jnp.bfloat16)


def phonon_sum(block, vectors, weights, q_points):
    phase_real, phase_imag = phases(q_points, vectors, weights)
    rows = block.shape[1]
    cells = block.shape[2]
    lanes = block.shape[3]
    flat_real = block[0].reshape(rows, cells * lanes)
    flat_imag = block[1].reshape(rows, cells * lanes)
    part_real = jnp.dot(phase_real, flat_real, preferred_element_type=jnp.float32) - jnp.dot(
        phase_imag, flat_imag, preferred_element_type=jnp.float32
    )
    part_imag = jnp.dot(phase_real, flat_imag, preferred_element_type=jnp.float32) + jnp.dot(
        phase_imag, flat_real, preferred_element_type=jnp.float32
    )
    return jnp.stack([part_real, part_imag]).reshape(2, q_points.shape[0], cells, lanes)


def per_device(
    coarse,
    rp_vectors,
    rp_weights,
    re_vectors,
    re_weights,
    q_points,
    k_points,
    modes_rot,
    u_k,
    u_kq,
    mask_k,
    mask_kq,
):
    q_count = q_points.shape[0]
    k_count = k_points.shape[0]
    band_count = u_k.shape[2]
    all_vectors, all_weights = (
        lax.all_gather(rp_vectors, "lat", axis=0, tiled=True),
        lax.all_gather(rp_weights, "lat", axis=0, tiled=True),
    )
    blocks = lax.all_to_all(coarse, "lat", split_axis=2, concat_axis=1, tiled=True)
    summed = phonon_sum(blocks, all_vectors, all_weights, q_points).astype(jnp.bfloat16)
    rotated = rotate_modes(summed, modes_rot)
    shared = lax.all_to_all(rotated, "lat", split_axis=3, concat_axis=2, tiled=True)
    lane_local = shared.shape[3]
    portion = lax.all_gather(shared, "kpt", axis=2, tiled=True)
    kreal, kimag = phases(k_points, re_vectors, re_weights)
    er = jnp.einsum(
        "kr,qrx->kqx", kreal, portion[0], preferred_element_type=jnp.float32
    ) - jnp.einsum("kr,qrx->kqx", kimag, portion[1], preferred_element_type=jnp.float32)
    ei = jnp.einsum(
        "kr,qrx->kqx", kreal, portion[1], preferred_element_type=jnp.float32
    ) + jnp.einsum("kr,qrx->kqx", kimag, portion[0], preferred_element_type=jnp.float32)
    totals = jnp.stack([er, ei])
    mode_local = lane_local // (band_count * band_count)
    field = totals.astype(jnp.bfloat16).reshape(
        2, k_count, q_count, mode_local, band_count, band_count
    )
    tr = jnp.einsum(
        "kqmab,kbn->kqman", field[0], u_k[0], preferred_element_type=jnp.float32
    ) - jnp.einsum("kqmab,kbn->kqman", field[1], u_k[1], preferred_element_type=jnp.float32)
    ti = jnp.einsum(
        "kqmab,kbn->kqman", field[0], u_k[1], preferred_element_type=jnp.float32
    ) + jnp.einsum("kqmab,kbn->kqman", field[1], u_k[0], preferred_element_type=jnp.float32)
    tr = tr.astype(jnp.bfloat16)
    ti = ti.astype(jnp.bfloat16)
    outr = jnp.einsum(
        "qkac,kqman->kqmcn", u_kq[0], tr, preferred_element_type=jnp.float32
    ) + jnp.einsum("qkac,kqman->kqmcn", u_kq[1], ti, preferred_element_type=jnp.float32)
    outi = jnp.einsum(
        "qkac,kqman->kqmcn", u_kq[0], ti, preferred_element_type=jnp.float32
    ) - jnp.einsum("qkac,kqman->kqmcn", u_kq[1], tr, preferred_element_type=jnp.float32)
    window = (
        jnp.transpose(mask_kq.astype(jnp.float32), (1, 0, 2))[:, :, None, :, None]
        * mask_k.astype(jnp.float32)[:, None, None, None, :]
    )
    result = jnp.stack([outr * window, outi * window])
    return result.reshape(2, k_count, q_count, lane_local).astype(jnp.bfloat16)


def solution(mesh):
    placed = (
        P(None, "lat", "kpt", None),
        P("lat", None),
        P("lat"),
        P(),
        P(),
        P(),
        P("kpt", None),
        P(),
        P(None, "kpt", None, None),
        P(None, None, "kpt", None, None),
        P("kpt", None),
        P(None, "kpt", None),
    )
    return jax.shard_map(
        per_device,
        mesh=mesh,
        in_specs=placed,
        out_specs=P(None, "kpt", None, "lat"),
        check_vma=False,
    )
```

profile of v0, /device:TPU:0, one launch (start us, length us, event | category | flops | bytes accessed | tf_op | source)
XLA Modules:
  0.0 252.8 jit_solution(12334398810767427954)
XLA Ops:
  0.7 1.8 copy.132
  2.5 1.2 dynamic-slice
  4.4 5.2 %all-to-all-start = ((bf16[2,1,4,12288]{3,0,1,2:T(2,128)(2,1)}), bf16[2,1,4,12288]{3,0,1,2:T(2,128)(2,1)S(1)}, u32[]{:S(2)}, u32[]{:S(2)}) async-start(bf16[2,1,4,12288]{3,0,1,2:T(2,128)(2,1)} %copy.132), calls=%async_computation | async-start | bytes 393216 | tf_op jit(solution)/shard_map/all_to_all | solution.py:73
  9.6 7.9 %all-reduce = s32[4]{0:T(128)S(1)} all-reduce(s32[4]{0:T(128)S(1)} %dynamic-update-slice), channel_id=1, replica_groups=mesh['lat'=4,'kpt'=8] {'lat'}, use_global_device_ids=true, to_apply=%add | all-reduce | flops 4 | bytes 32
  19.3 7.8 %all-gather = s32[4,1,3]{2,1,0:T(1,128)S(1)} all-gather(s32[1,1,3]{2,1,0:T(1,128)} %bitcast.155), channel_id=1, replica_groups=mesh['lat'=4,'kpt'=8] {'lat'}, dimensions={0}, use_global_device_ids=true | all-gather | bytes 60 | tf_op jit(solution)/shard_map/all_gather | solution.py:70
  37.3 10.0 %copy.135 = bf16[2,2,1,12288]{1,0,2,3:T(2,128)(2,1)} copy(bf16[2,2,1,12288]{3,1,2,0:T(2,128)(2,1)S(1)} %pad_maximum_fusion.1) | data formatting | bytes 196608 | tf_op jit(solution)/shard_map/stack | solution.py:33
  47.3 11.9 %reshape.167 = bf16[4,2,6144]{2,1,0:T(2,128)(2,1)} reshape(bf16[12288,1,2,2]{3,2,1,0:T(2,128)(2,1)} %bitcast.144) | data formatting | bytes 196608
  59.3 3.3 %all-to-all-start.1 = ((bf16[4,2,6144]{2,1,0:T(2,128)(2,1)}), bf16[4,2,6144]{2,1,0:T(2,128)(2,1)S(1)}, u32[]{:S(2)}, u32[]{:S(2)}) async-start(bf16[4,2,6144]{2,1,0:T(2,128)(2,1)} %reshape.167), calls=%async_computation.1 | async-start | bytes 196608 | tf_op jit(solution)/shard_map/all_to_all | solution.py:76
  65.4 2.1 all-to-all-done.1
  67.5 14.7 %reshape.168 = bf16[12288,1,2,2]{3,2,1,0:T(2,128)(2,1)} reshape(bf16[4,2,6144]{2,1,0:T(2,128)(2,1)S(1)} %all-to-all-done.1) | data formatting | bytes 196608
  82.2 12.7 %copy.137 = bf16[2,2,4,3072]{3,1,0,2:T(2,128)(2,1)S(1)} copy(bf16[2,2,4,3072]{1,0,3,2:T(2,128)(2,1)} %bitcast.145) | data formatting | bytes 196608 | tf_op jit(solution)/shard_map/all_to_all | solution.py:76
  94.8 16.5 %all_gather.11 = bf16[2,2,32,3072]{3,1,0,2:T(2,128)(2,1)S(1)} all-gather(bf16[2,2,4,3072]{3,1,0,2:T(2,128)(2,1)S(1)} %copy.137), channel_id=1, replica_groups=mesh['lat'=4,'kpt'=8] {'kpt'}, dimensions={2}, use_global_device_ids=true | all-gather | bytes 884736 | tf_op jit(solution)/shard_map/all_gather | solution.py:78
  112.9 1.4 fusion.3
  114.4 2.4 copy.143
  116.8 1.4 fusion.2
  118.2 1.8 copy.140
  120.0 9.8 %copy.142 = bf16[64,2,12,16,16]{4,3,2,1,0:T(8,128)(2,1)} copy(bf16[64,2,12,16,16]{0,4,3,2,1:T(8,128)(2,1)S(1)} %bitcast.147) | data formatting | bytes 1572864 | tf_op jit(solution)/shard_map/squeeze | solution.py:92
  129.8 10.8 %copy.145 = bf16[64,2,12,16,16]{4,3,2,1,0:T(8,128)(2,1)} copy(bf16[64,2,12,16,16]{0,4,3,2,1:T(8,128)(2,1)} %bitcast.146) | data formatting | bytes 1572864 | tf_op jit(solution)/shard_map/squeeze | solution.py:93
  140.6 9.2 %fusion.23 = f32[64,2,12,16,16]{4,3,2,1,0:T(8,128)} fusion(bf16[64,2,12,16,16]{4,3,2,1,0:T(8,128)(2,1)} %copy.142, bf16[1,64,16,16]{3,2,1,0:T(8,128)(2,1)} %copy.176), kind=kOutput, calls=%fused_computation.36 | convolution fusion | flops 12582912 | bytes 2392064 | tf_op jit(solution)/shard_map/kqmab,kbn->kqman/dot_general | solution.py:94
  149.8 5.5 %fusion.21 = f32[64,2,12,16,16]{4,3,2,1,0:T(8,128)} fusion(bf16[64,2,12,16,16]{4,3,2,1,0:T(8,128)(2,1)S(1)} %bitcast.143, bf16[1,64,16,16]{3,2,1,0:T(8,128)(2,1)S(1)} %copy.175), kind=kOutput, calls=%fused_computation.34 | convolution fusion | flops 12582912 | bytes 2392064 | tf_op jit(solution)/shard_map/kqmab,kbn->kqman/dot_general | solution.py:91
  155.3 8.2 %add_convert_fusion = bf16[64,2,12,16,16]{4,3,2,1,0:T(8,128)(2,1)S(1)} fusion(f32[64,2,12,16,16]{4,3,2,1,0:T(8,128)} %fusion.23, bf16[64,2,12,16,16]{4,3,2,1,0:T(8,128)(2,1)} %copy.145, bf16[1,64,16,16]{3,2,1,0:T(8,128)(2,1)S(1)} %copy.175), kind=kOutput, calls=%fused_computation.4 | convolution fusion | flops 13369344 | bytes 3178496 | tf_op jit(solution)/shard_map/kqmab,kbn->kqman/dot_general | solution.py:96
  163.5 10.9 %subtract_convert_fusion = bf16[64,2,12,16,16]{4,3,2,1,0:T(8,128)(2,1)} fusion(f32[64,2,12,16,16]{4,3,2,1,0:T(8,128)} %fusion.21, bf16[64,2,12,16,16]{4,3,2,1,0:T(8,128)(2,1)} %copy.145, bf16[1,64,16,16]{3,2,1,0:T(8,128)(2,1)S(1)} %copy-done.1), kind=kOutput, calls=%fused_computation.5 | convolution fusion | flops 13369344 | bytes 3178496 | tf_op jit(solution)/shard_map/kqmab,kbn->kqman/dot_general | solution.py:93
  174.4 9.7 %fusion.10 = f32[64,2,12,16,16]{4,3,2,1,0:T(8,128)} fusion(bf16[64,2,12,16,16]{4,3,2,1,0:T(8,128)(2,1)} %subtract_convert_fusion, bf16[1,2,64,16,16]{4,3,1,2,0:T(8,128)(2,1)S(1)} %copy.178), kind=kOutput, calls=%fused_computation.21 | convolution fusion | flops 12582912 | bytes 2424832 | tf_op jit(solution)/shard_map/qkac,kqman->kqmcn/dot_general | solution.py:104
  184.1 5.7 %fusion.16 = f32[64,2,12,16,16]{4,3,2,1,0:T(8,128)} fusion(bf16[64,2,12,16,16]{4,3,2,1,0:T(8,128)(2,1)S(1)} %copy-done, bf16[1,2,64,16,16]{4,3,1,2,0:T(8,128)(2,1)S(1)} %copy.177), kind=kOutput, calls=%fused_computation.27 | convolution fusion | flops 12582912 | bytes 2424832 | tf_op jit(solution)/shard_map/qkac,kqman->kqmcn/dot_general | solution.py:99
  189.8 5.6 %fusion.14 = f32[64,2,12,16,16]{4,3,2,1,0:T(8,128)} fusion(bf16[64,2,12,16,16]{4,3,2,1,0:T(8,128)(2,1)S(1)} %add_convert_fusion, bf16[1,2,64,16,16]{4,3,1,2,0:T(8,128)(2,1)S(1)} %copy.177), kind=kOutput, calls=%fused_computation.25 | convolution fusion | flops 12582912 | bytes 2424832 | tf_op jit(solution)/shard_map/qkac,kqman->kqmcn/dot_general | solution.py:102
  195.5 5.8 %fusion.12 = f32[64,2,12,16,16]{4,3,2,1,0:T(8,128)} fusion(bf16[64,2,12,16,16]{4,3,2,1,0:T(8,128)(2,1)S(1)} %add_convert_fusion, bf16[1,2,64,16,16]{4,3,1,2,0:T(8,128)(2,1)S(1)} %copy.178), kind=kOutput, calls=%fused_computation.23 | convolution fusion | flops 12582912 | bytes 2424832 | tf_op jit(solution)/shard_map/qkac,kqman->kqmcn/dot_general | solution.py:101
  201.3 9.7 %copy.157 = f32[64,2,12,16,16]{0,3,4,2,1:T(8,128)S(1)} copy(f32[64,2,12,16,16]{4,3,2,1,0:T(8,128)} %fusion.10) | data formatting | bytes 3145728 | tf_op jit(solution)/shard_map/qkac,kqman->kqmcn/dot_general | solution.py:104
  211.0 10.9 %copy.152 = f32[64,2,12,16,16]{0,3,4,2,1:T(8,128)} copy(f32[64,2,12,16,16]{4,3,2,1,0:T(8,128)} %fusion.16) | data formatting | bytes 3145728 | tf_op jit(solution)/shard_map/qkac,kqman->kqmcn/dot_general | solution.py:99
  221.9 10.9 %copy.156 = f32[64,2,12,16,16]{0,3,4,2,1:T(8,128)} copy(f32[64,2,12,16,16]{4,3,2,1,0:T(8,128)} %fusion.14) | data formatting | bytes 3145728 | tf_op jit(solution)/shard_map/qkac,kqman->kqmcn/dot_general | solution.py:102
  232.8 10.9 %copy.153 = f32[64,2,12,16,16]{0,3,4,2,1:T(8,128)} copy(f32[64,2,12,16,16]{4,3,2,1,0:T(8,128)} %fusion.12) | data formatting | bytes 3145728 | tf_op jit(solution)/shard_map/qkac,kqman->kqmcn/dot_general | solution.py:101
  243.7 5.0 %fusion.5 = (bf16[64,2,12,16,16]{0,4,3,2,1:T(8,128)(2,1)S(1)}, bf16[64,2,12,16,16]{0,4,3,2,1:T(8,128)(2,1)S(1)}) fusion(f32[64,2,12,16,16]{0,3,4,2,1:T(8,128)} %copy.152, f32[64,2,12,16,16]{0,3,4,2,1:T(8,128)} %copy.153, f32[64,2,16,16]{0,3,2,1:T(8,128)S(1)} %copy-done.2, f32[64,2,12,16,16]{0,3,4,2,1:T(8,128)} %copy.156, f32[64,2,12,16,16]{0,3,4,2,1:T(8,128)S(1)} %copy.157), kind=kLoop, calls=%fused_computation.14 | loop fusion | flops 2359296 | bytes 7995392 | tf_op jit(solution)/shard_map/convert.3
  249.5 3.3 %copy.158 = bf16[2,64,2,3072]{3,2,1,0:T(2,128)(2,1)} copy(bf16[2,64,2,3072]{1,3,2,0:T(8,128)(2,1)S(1)} %pad_maximum_fusion) | data formatting | bytes 3145728 | tf_op jit(solution)/shard_map/stack | solution.py:109
  (50 shorter events, 17.7 us)
Async XLA Ops:
  4.4 27.8 %all-to-all-start = ((bf16[2,1,4,12288]{3,0,1,2:T(2,128)(2,1)}), bf16[2,1,4,12288]{3,0,1,2:T(2,128)(2,1)S(1)}, u32[]{:S(2)}, u32[]{:S(2)}) async-start(bf16[2,1,4,12288]{3,0,1,2:T(2,128)(2,1)} %copy.132), calls=%async_computation | async-start | bytes 393216 | tf_op jit(solution)/shard_map/all_to_all | solution.py:73
  37.3 25.3 %copy-start.3 = (s32[32]{0:T(128)S(1)}, s32[32]{0:T(128)}, u32[]{:S(2)}) copy-start(s32[32]{0:T(128)} %param.16) | copy-start | bytes 388
  59.3 8.2 %all-to-all-start.1 = ((bf16[4,2,6144]{2,1,0:T(2,128)(2,1)}), bf16[4,2,6144]{2,1,0:T(2,128)(2,1)S(1)}, u32[]{:S(2)}, u32[]{:S(2)}) async-start(bf16[4,2,6144]{2,1,0:T(2,128)(2,1)} %reshape.167), calls=%async_computation.1 | async-start | bytes 196608 | tf_op jit(solution)/shard_map/all_to_all | solution.py:76
  129.8 20.0 %slice-start = ((s8[6291456]{0:T(1024)(128)(4,1)}), s8[2097152]{0:T(1024)(128)(4,1)S(1)}, s32[]{:S(2)}) async-start(s8[6291456]{0:T(1024)(128)(4,1)} %bitcast.142), calls=%async_computation.2 | async-start | bytes 4194304
  140.6 9.2 %slice-start.1 = ((s8[6291456]{0:T(1024)(128)(4,1)}), s8[4194304]{0:T(1024)(128)(4,1)S(1)}, s32[]{:S(2)}) async-start(s8[6291456]{0:T(1024)(128)(4,1)} %bitcast.142), calls=%async_computation.3 | async-start | bytes 8388608
  155.3 8.2 %copy-start.1 = (bf16[1,64,16,16]{3,2,1,0:T(8,128)(2,1)S(1)}, bf16[1,64,16,16]{3,2,1,0:T(8,128)(2,1)}, u32[]{:S(2)}) copy-start(bf16[1,64,16,16]{3,2,1,0:T(8,128)(2,1)} %copy.176) | copy-start | bytes 98308
  174.4 9.7 %copy-start = (bf16[64,2,12,16,16]{4,3,2,1,0:T(8,128)(2,1)S(1)}, bf16[64,2,12,16,16]{4,3,2,1,0:T(8,128)(2,1)}, u32[]{:S(2)}) copy-start(bf16[64,2,12,16,16]{4,3,2,1,0:T(8,128)(2,1)} %subtract_convert_fusion) | copy-start | bytes 2359300
  232.8 10.9 %copy-start.2 = (f32[64,2,16,16]{0,3,2,1:T(8,128)S(1)}, f32[64,2,16,16]{0,3,2,1:T(8,128)}, u32[]{:S(2)}) copy-start(f32[64,2,16,16]{0,3,2,1:T(8,128)} %broadcast_multiply_fusion) | copy-start | bytes 393220
where the time goes:
time: 254 us; the launch traced here: 253 us
  local copies, waits for them, and re-layouts  131 us (52%)
  matrix products  69.2 us (27%)
  blocking collectives  32.2 us (13%)
  other arithmetic  8.81 us (3%)
  starting transfers between devices  8.5 us (3%)
    unnamed x22, local copies, waits for them, and re-layouts  33.1 us
    all_gather x1, blocking collectives, per_device(): portion = lax.all_gather(shared, 'kpt', axis=2, tiled=True)  16.5 us
    all_to_all x1, local copies, waits for them, and re-layouts, per_device(): lax.all_to_all(rotated, 'lat', split_axis=3, concat_axis=2, tiled=True)  12.7 us
    dot_general x1, local copies, waits for them, and re-layouts, per_device(): jnp.einsum('qkac,kqman->kqmcn', u_kq[1], ti, preferred_element_type=jnp.f...  10.9 us
    dot_general x1, local copies, waits for them, and re-layouts, per_device(): jnp.einsum('qkac,kqman->kqmcn', u_kq[0], tr, preferred_element_type=jnp.f...  10.9 us
    dot_general x1, local copies, waits for them, and re-layouts, per_device(): jnp.einsum('qkac,kqman->kqmcn', u_kq[0], ti, preferred_element_type=jnp.f...  10.9 us
    dot_general x1, matrix products, per_device(): jnp.einsum('kqmab,kbn->kqman', field[1], u_k[1], preferred_element_type=j...  10.9 us
    squeeze x1, local copies, waits for them, and re-layouts, per_device(): field[1]  10.8 us
  transfers between devices with their start and end apart: 2, of which 1 were waited for; matrix products, arithmetic and copies ran while one was open for 4% of the time, Pallas kernels for 0%

commit v1 on v0

--- a/solution.py
+++ b/solution.py
@@ -75,7 +75,7 @@
     rotated = rotate_modes(summed, modes_rot)
     shared = lax.all_to_all(rotated, "lat", split_axis=3, concat_axis=2, tiled=True)
     lane_local = shared.shape[3]
-    portion = lax.all_gather(shared, "kpt", axis=2, tiled=True)
+    portion = jnp.concatenate(jax.lax.all_gather(shared, "kpt"), axis=2)
     kreal, kimag = phases(k_points, re_vectors, re_weights)
     er = jnp.einsum(
         "kr,qrx->kqx", kreal, portion[0], preferred_element_type=jnp.float32

time: 254 us -> 257 us (1.012)
  local copies, waits for them, and re-layouts: 131 us -> 135 us
    all_gather x0 -> x1, local copies, waits for them, and re-layouts: none -> 14.5 us  [per_device(): portion = jnp.concatenate(jax.lax.all_gather(shared, 'kpt'), axis=2)]
    all_to_all x1 -> x0, local copies, waits for them, and re-layouts: 12.7 us -> none  [per_device(): lax.all_to_all(rotated, 'lat', split_axis=3, concat_axis=2, tiled=True)]
    unnamed x22 -> x24, local copies, waits for them, and re-layouts: 33.1 us -> 34 us
where the time goes in v1:
time: 257 us; the launch traced here: 255 us
  local copies, waits for them, and re-layouts  135 us (53%)
  matrix products  68.4 us (27%)
  blocking collectives  32.2 us (13%)
  other arithmetic  8.8 us (3%)
  starting transfers between devices  8.5 us (3%)
    unnamed x24, local copies, waits for them, and re-layouts  34 us
    all_gather x1, blocking collectives, per_device(): portion = jnp.concatenate(jax.lax.all_gather(shared, 'kpt'), axis=2)  16.5 us
    all_gather x1, local copies, waits for them, and re-layouts, per_device(): portion = jnp.concatenate(jax.lax.all_gather(shared, 'kpt'), axis=2)  14.5 us
    dot_general x1, local copies, waits for them, and re-layouts, per_device(): jnp.einsum('qkac,kqman->kqmcn', u_kq[1], ti, preferred_element_type=jnp.f...  10.9 us
    dot_general x1, local copies, waits for them, and re-layouts, per_device(): jnp.einsum('qkac,kqman->kqmcn', u_kq[0], tr, preferred_element_type=jnp.f...  10.9 us
    dot_general x1, local copies, waits for them, and re-layouts, per_device(): jnp.einsum('qkac,kqman->kqmcn', u_kq[0], ti, preferred_element_type=jnp.f...  10.9 us
    dot_general x1, matrix products, per_device(): jnp.einsum('kqmab,kbn->kqman', field[1], u_k[1], preferred_element_type=j...  10.9 us
    squeeze x1, local copies, waits for them, and re-layouts, per_device(): field[1]  10.7 us
  transfers between devices with their start and end apart: 2, of which 1 were waited for; matrix products, arithmetic and copies ran while one was open for 4% of the time, Pallas kernels for 0%

profile of v1, /device:TPU:0, one launch (start us, length us, event | category | flops | bytes accessed | tf_op | source)
XLA Modules:
  0.0 254.8 jit_solution(788951968877897935)
XLA Ops:
  0.7 1.8 copy.130
  2.5 1.3 dynamic-slice
  4.6 5.2 %all-to-all-start = ((bf16[2,1,4,12288]{3,0,1,2:T(2,128)(2,1)}), bf16[2,1,4,12288]{3,0,1,2:T(2,128)(2,1)S(1)}, u32[]{:S(2)}, u32[]{:S(2)}) async-start(bf16[2,1,4,12288]{3,0,1,2:T(2,128)(2,1)} %copy.130), calls=%async_computation | async-start | bytes 393216 | tf_op jit(solution)/shard_map/all_to_all | solution.py:73
  9.8 7.9 %all-reduce = s32[4]{0:T(128)S(1)} all-reduce(s32[4]{0:T(128)S(1)} %dynamic-update-slice), channel_id=1, replica_groups=mesh['lat'=4,'kpt'=8] {'lat'}, use_global_device_ids=true, to_apply=%add | all-reduce | flops 4 | bytes 32
  19.5 7.8 %all-gather = s32[4,1,3]{2,1,0:T(1,128)S(1)} all-gather(s32[1,1,3]{2,1,0:T(1,128)} %bitcast.151), channel_id=1, replica_groups=mesh['lat'=4,'kpt'=8] {'lat'}, dimensions={0}, use_global_device_ids=true | all-gather | bytes 60 | tf_op jit(solution)/shard_map/all_gather | solution.py:70
  37.5 10.0 %copy.133 = bf16[2,2,1,12288]{1,0,2,3:T(2,128)(2,1)} copy(bf16[2,2,1,12288]{3,1,2,0:T(2,128)(2,1)S(1)} %pad_maximum_fusion.1) | data formatting | bytes 196608 | tf_op jit(solution)/shard_map/stack | solution.py:33
  47.5 11.9 %reshape.177 = bf16[4,2,6144]{2,1,0:T(2,128)(2,1)} reshape(bf16[12288,1,2,2]{3,2,1,0:T(2,128)(2,1)} %bitcast.139) | data formatting | bytes 196608
  59.4 3.3 %all-to-all-start.1 = ((bf16[4,2,6144]{2,1,0:T(2,128)(2,1)}), bf16[4,2,6144]{2,1,0:T(2,128)(2,1)S(1)}, u32[]{:S(2)}, u32[]{:S(2)}) async-start(bf16[4,2,6144]{2,1,0:T(2,128)(2,1)} %reshape.177), calls=%async_computation.1 | async-start | bytes 196608 | tf_op jit(solution)/shard_map/all_to_all | solution.py:76
  66.2 1.4 all-to-all-done.1
  67.6 14.7 %reshape.178 = bf16[12288,1,2,2]{3,2,1,0:T(2,128)(2,1)} reshape(bf16[4,2,6144]{2,1,0:T(2,128)(2,1)S(1)} %all-to-all-done.1) | data formatting | bytes 196608
  82.3 14.5 %copy.164 = bf16[1,2,2,4,3072]{4,3,2,1,0:T(4,128)(2,1)S(1)} copy(bf16[1,2,2,4,3072]{2,1,4,3,0:T(2,128)(2,1)} %bitcast.140) | data formatting | bytes 196608 | tf_op jit(solution)/shard_map/all_gather | solution.py:78
  96.8 16.5 %all_gather.15 = bf16[8,2,2,4,3072]{4,3,2,1,0:T(4,128)(2,1)S(1)} all-gather(bf16[1,2,2,4,3072]{4,3,2,1,0:T(4,128)(2,1)S(1)} %copy.164), channel_id=1, replica_groups=mesh['lat'=4,'kpt'=8] {'kpt'}, dimensions={0}, use_global_device_ids=true | all-gather | bytes 884736 | tf_op jit(solution)/shard_map/all_gather | solution.py:78
  115.1 1.4 fusion.2
  116.6 2.4 copy.137
  119.0 1.4 fusion.3
  120.4 2.6 %copy.140 = bf16[64,2,3072]{0,2,1:T(8,128)(2,1)} copy(bf16[64,2,3072]{2,0,1:T(8,128)(2,1)} %fusion.3) | data formatting | bytes 1572864 | tf_op jit(solution)/shard_map/convert.6
  123.0 10.7 %copy.142 = bf16[64,2,12,16,16]{4,3,2,1,0:T(8,128)(2,1)} copy(bf16[64,2,12,16,16]{0,4,3,2,1:T(8,128)(2,1)} %bitcast.142) | data formatting | bytes 1572864 | tf_op jit(solution)/shard_map/squeeze | solution.py:93
  133.7 9.8 %copy.139 = bf16[64,2,12,16,16]{4,3,2,1,0:T(8,128)(2,1)} copy(bf16[64,2,12,16,16]{0,4,3,2,1:T(8,128)(2,1)S(1)} %bitcast.141) | data formatting | bytes 1572864 | tf_op jit(solution)/shard_map/squeeze | solution.py:92
  143.5 9.2 %fusion.21 = f32[64,2,12,16,16]{4,3,2,1,0:T(8,128)} fusion(bf16[64,2,12,16,16]{4,3,2,1,0:T(8,128)(2,1)} %copy.139, bf16[1,64,16,16]{3,2,1,0:T(8,128)(2,1)S(1)} %copy-done.4), kind=kOutput, calls=%fused_computation.32 | convolution fusion | flops 12582912 | bytes 2392064 | tf_op jit(solution)/shard_map/kqmab,kbn->kqman/dot_general | solution.py:94
  152.7 5.5 %fusion.19 = f32[64,2,12,16,16]{4,3,2,1,0:T(8,128)} fusion(bf16[64,2,12,16,16]{4,3,2,1,0:T(8,128)(2,1)S(1)} %copy-done.1, bf16[1,64,16,16]{3,2,1,0:T(8,128)(2,1)S(1)} %copy-done.3), kind=kOutput, calls=%fused_computation.30 | convolution fusion | flops 12582912 | bytes 2392064 | tf_op jit(solution)/shard_map/kqmab,kbn->kqman/dot_general | solution.py:91
  158.2 8.2 %add_convert_fusion = bf16[64,2,12,16,16]{4,3,2,1,0:T(8,128)(2,1)S(1)} fusion(f32[64,2,12,16,16]{4,3,2,1,0:T(8,128)} %fusion.21, bf16[64,2,12,16,16]{4,3,2,1,0:T(8,128)(2,1)} %copy.142, bf16[1,64,16,16]{3,2,1,0:T(8,128)(2,1)S(1)} %copy-done.3), kind=kOutput, calls=%fused_computation.4 | convolution fusion | flops 13369344 | bytes 3178496 | tf_op jit(solution)/shard_map/kqmab,kbn->kqman/dot_general | solution.py:96
  166.4 10.9 %subtract_convert_fusion = bf16[64,2,12,16,16]{4,3,2,1,0:T(8,128)(2,1)} fusion(f32[64,2,12,16,16]{4,3,2,1,0:T(8,128)} %fusion.19, bf16[64,2,12,16,16]{4,3,2,1,0:T(8,128)(2,1)} %copy.142, bf16[1,64,16,16]{3,2,1,0:T(8,128)(2,1)S(1)} %copy-done.4), kind=kOutput, calls=%fused_computation.5 | convolution fusion | flops 13369344 | bytes 3178496 | tf_op jit(solution)/shard_map/kqmab,kbn->kqman/dot_general | solution.py:93
  177.3 9.6 %fusion.10 = f32[64,2,12,16,16]{4,3,2,1,0:T(8,128)} fusion(bf16[64,2,12,16,16]{4,3,2,1,0:T(8,128)(2,1)} %subtract_convert_fusion, bf16[1,2,64,16,16]{4,3,1,2,0:T(8,128)(2,1)S(1)} %copy.172), kind=kOutput, calls=%fused_computation.21 | convolution fusion | flops 12582912 | bytes 2424832 | tf_op jit(solution)/shard_map/qkac,kqman->kqmcn/dot_general | solution.py:104
  186.8 5.5 %fusion.16 = f32[64,2,12,16,16]{4,3,2,1,0:T(8,128)} fusion(bf16[64,2,12,16,16]{4,3,2,1,0:T(8,128)(2,1)S(1)} %copy-done, bf16[1,2,64,16,16]{4,3,1,2,0:T(8,128)(2,1)S(1)} %copy.171), kind=kOutput, calls=%fused_computation.27 | convolution fusion | flops 12582912 | bytes 2424832 | tf_op jit(solution)/shard_map/qkac,kqman->kqmcn/dot_general | solution.py:99
  192.3 5.5 %fusion.14 = f32[64,2,12,16,16]{4,3,2,1,0:T(8,128)} fusion(bf16[64,2,12,16,16]{4,3,2,1,0:T(8,128)(2,1)S(1)} %add_convert_fusion, bf16[1,2,64,16,16]{4,3,1,2,0:T(8,128)(2,1)S(1)} %copy.171), kind=kOutput, calls=%fused_computation.25 | convolution fusion | flops 12582912 | bytes 2424832 | tf_op jit(solution)/shard_map/qkac,kqman->kqmcn/dot_general | solution.py:102
  197.8 5.5 %fusion.12 = f32[64,2,12,16,16]{4,3,2,1,0:T(8,128)} fusion(bf16[64,2,12,16,16]{4,3,2,1,0:T(8,128)(2,1)S(1)} %add_convert_fusion, bf16[1,2,64,16,16]{4,3,1,2,0:T(8,128)(2,1)S(1)} %copy.172), kind=kOutput, calls=%fused_computation.23 | convolution fusion | flops 12582912 | bytes 2424832 | tf_op jit(solution)/shard_map/qkac,kqman->kqmcn/dot_general | solution.py:101
  203.3 9.7 %copy.154 = f32[64,2,12,16,16]{0,3,4,2,1:T(8,128)S(1)} copy(f32[64,2,12,16,16]{4,3,2,1,0:T(8,128)} %fusion.10) | data formatting | bytes 3145728 | tf_op jit(solution)/shard_map/qkac,kqman->kqmcn/dot_general | solution.py:104
  213.0 10.9 %copy.149 = f32[64,2,12,16,16]{0,3,4,2,1:T(8,128)} copy(f32[64,2,12,16,16]{4,3,2,1,0:T(8,128)} %fusion.16) | data formatting | bytes 3145728 | tf_op jit(solution)/shard_map/qkac,kqman->kqmcn/dot_general | solution.py:99
  223.9 10.9 %copy.153 = f32[64,2,12,16,16]{0,3,4,2,1:T(8,128)} copy(f32[64,2,12,16,16]{4,3,2,1,0:T(8,128)} %fusion.14) | data formatting | bytes 3145728 | tf_op jit(solution)/shard_map/qkac,kqman->kqmcn/dot_general | solution.py:102
  234.8 10.9 %copy.150 = f32[64,2,12,16,16]{0,3,4,2,1:T(8,128)} copy(f32[64,2,12,16,16]{4,3,2,1,0:T(8,128)} %fusion.12) | data formatting | bytes 3145728 | tf_op jit(solution)/shard_map/qkac,kqman->kqmcn/dot_general | solution.py:101
  245.7 5.0 %fusion.5 = (bf16[64,2,12,16,16]{0,4,3,2,1:T(8,128)(2,1)S(1)}, bf16[64,2,12,16,16]{0,4,3,2,1:T(8,128)(2,1)S(1)}) fusion(f32[64,2,12,16,16]{0,3,4,2,1:T(8,128)} %copy.149, f32[64,2,12,16,16]{0,3,4,2,1:T(8,128)} %copy.150, f32[64,2,16,16]{0,3,2,1:T(8,128)S(1)} %copy-done.5, f32[64,2,12,16,16]{0,3,4,2,1:T(8,128)} %copy.153, f32[64,2,12,16,16]{0,3,4,2,1:T(8,128)S(1)} %copy.154), kind=kLoop, calls=%fused_computation.14 | loop fusion | flops 2359296 | bytes 7995392 | tf_op jit(solution)/shard_map/convert.3
  251.5 3.3 %copy.155 = bf16[2,64,2,3072]{3,2,1,0:T(2,128)(2,1)} copy(bf16[2,64,2,3072]{1,3,2,0:T(8,128)(2,1)S(1)} %pad_maximum_fusion) | data formatting | bytes 3145728 | tf_op jit(solution)/shard_map/stack | solution.py:109
  (55 shorter events, 18.7 us)
Async XLA Ops:
  4.6 27.7 %all-to-all-start = ((bf16[2,1,4,12288]{3,0,1,2:T(2,128)(2,1)}), bf16[2,1,4,12288]{3,0,1,2:T(2,128)(2,1)S(1)}, u32[]{:S(2)}, u32[]{:S(2)}) async-start(bf16[2,1,4,12288]{3,0,1,2:T(2,128)(2,1)} %copy.130), calls=%async_computation | async-start | bytes 393216 | tf_op jit(solution)/shard_map/all_to_all | solution.py:73
  37.5 25.2 %copy-start.6 = (s32[32]{0:T(128)S(1)}, s32[32]{0:T(128)}, u32[]{:S(2)}) copy-start(s32[32]{0:T(128)} %param.16) | copy-start | bytes 388
  59.4 8.2 %all-to-all-start.1 = ((bf16[4,2,6144]{2,1,0:T(2,128)(2,1)}), bf16[4,2,6144]{2,1,0:T(2,128)(2,1)S(1)}, u32[]{:S(2)}, u32[]{:S(2)}) async-start(bf16[4,2,6144]{2,1,0:T(2,128)(2,1)} %reshape.177), calls=%async_computation.1 | async-start | bytes 196608 | tf_op jit(solution)/shard_map/all_to_all | solution.py:76
  120.4 13.3 %copy-start.2 = (bf16[64,2,3072]{0,2,1:T(8,128)(2,1)S(1)}, bf16[64,2,3072]{0,2,1:T(8,128)(2,1)}, u32[]{:S(2)}) copy-start(bf16[64,2,3072]{0,2,1:T(8,128)(2,1)} %copy.137) | copy-start | bytes 2359300
  123.0 20.5 %copy-start.4 = (bf16[1,64,16,16]{3,2,1,0:T(8,128)(2,1)S(1)}, bf16[1,64,16,16]{3,2,1,0:T(8,128)(2,1)}, u32[]{:S(2)}) copy-start(bf16[1,64,16,16]{3,2,1,0:T(8,128)(2,1)} %copy.170) | copy-start | bytes 98308
  143.5 9.2 %copy-start.1 = (bf16[64,2,12,16,16]{4,3,2,1,0:T(8,128)(2,1)S(1)}, bf16[64,2,12,16,16]{4,3,2,1,0:T(8,128)(2,1)}, u32[]{:S(2)}) copy-start(bf16[64,2,12,16,16]{4,3,2,1,0:T(8,128)(2,1)} %copy.139) | copy-start | bytes 2359300
  143.5 9.2 %copy-start.3 = (bf16[1,64,16,16]{3,2,1,0:T(8,128)(2,1)S(1)}, bf16[1,64,16,16]{3,2,1,0:T(8,128)(2,1)}, u32[]{:S(2)}) copy-start(bf16[1,64,16,16]{3,2,1,0:T(8,128)(2,1)} %copy.169) | copy-start | bytes 98308
  177.2 9.6 %copy-start = (bf16[64,2,12,16,16]{4,3,2,1,0:T(8,128)(2,1)S(1)}, bf16[64,2,12,16,16]{4,3,2,1,0:T(8,128)(2,1)}, u32[]{:S(2)}) copy-start(bf16[64,2,12,16,16]{4,3,2,1,0:T(8,128)(2,1)} %subtract_convert_fusion) | copy-start | bytes 2359300
  234.8 10.9 %copy-start.5 = (f32[64,2,16,16]{0,3,2,1:T(8,128)S(1)}, f32[64,2,16,16]{0,3,2,1:T(8,128)}, u32[]{:S(2)}) copy-start(f32[64,2,16,16]{0,3,2,1:T(8,128)} %broadcast_multiply_fusion) | copy-start | bytes 393220
